TPU v7x, 32 devices: a whole 2x2x4 slice. The times are simulated.
32 devices in a mesh: dp: 2 (over core), row: 4 (over y, x), col: 4 (over z).
Axes of the slice: x: 2, y: 2, z: 4, core: 2. Of those that a mesh axis runs over, the one named last changes fastest.
Arguments:
- inputs: bfloat16 [32768, 768], P(('dp', 'row', 'col')), may hold values from -6 to 6
- segment_ids: int32 [32768], P(('dp', 'row', 'col')), may hold values from 0 to 3, as said below
- query_weight: bfloat16 [768, 768], P('row', 'col'), may hold values from -0.21875 to 0.21875
- key_weight: bfloat16 [768, 768], P('row', 'col'), may hold values from -0.21875 to 0.21875
- value_weight: bfloat16 [768, 768], P('row', 'col'), may hold values from -0.21875 to 0.21875
- output_weight: bfloat16 [768, 768], P('row', 'col'), may hold values from -1.75 to 1.75
- gate_weight: bfloat16 [768, 2048], P('row', 'col'), may hold values from -0.21875 to 0.21875
- up_weight: bfloat16 [768, 2048], P('row', 'col'), may hold values from -0.21875 to 0.21875
- down_weight: bfloat16 [2048, 768], P('row', 'col'), may hold values from -0.125 to 0.125
- first_gain: bfloat16 [768], P(('row', 'col')), may hold values from 0.099609375 to 1.8984375
- second_gain: bfloat16 [768], P(('row', 'col')), may hold values from 0.099609375 to 1.8984375
- cotangent: bfloat16 [32768, 768], P(('dp', 'row', 'col')), may hold values from -6 to 6
Outputs:
- layer_out: bfloat16 [32768, 768], P(('dp', 'row', 'col'))
- input_grad: bfloat16 [32768, 768], P(('dp', 'row', 'col'))
- query_grad: float32 [768, 768], P('row', 'col')
- key_grad: float32 [768, 768], P('row', 'col')
- value_grad: float32 [768, 768], P('row', 'col')
- output_grad: float32 [768, 768], P('row', 'col')
- gate_grad: float32 [768, 2048], P('row', 'col')
- up_grad: float32 [768, 2048], P('row', 'col')
- down_grad: float32 [2048, 768], P('row', 'col')
- first_gain_grad: float32 [768], P(('row', 'col'))
- second_gain_grad: float32 [768], P(('row', 'col'))
Inputs may be any that keep to these rules, and one draw needn't show every extreme that they name: `segment_ids`: within each aligned block of 1024 tokens the ids number that block's sequences 0, 1, ... in order; a block holds 1, 2 or 4 sequences of equal length, and each of the three cases occurs in some block.
All inputs are finite; a program needn't handle non-finite values.
Results may differ from a plain program's by a relative error of at most 0.017.
Values may be sent and summed in bfloat16 or wider, within the bound.
No kernel may reach another device: no remote copies, remote signals or barrier semaphores. Data moves between devices by JAX's collectives and lax.ppermute only.
A program may use at most 192 MiB of HBM per device.

v0:
```python
import jax
import jax.numpy as jnp
from jax import lax
from jax.sharding import PartitionSpec as P

HEAD_DIM = 64
EPSILON = 1e-06
ROPE_BASE = 10000.0
NEGATIVE = -1e30


def for_sending(value):

    def short(part):
        return part.astype(jnp.bfloat16) if part.dtype == jnp.float32 else part

    return jax.tree.map(short, value)


def assemble(stack, grid_rows, grid_cols):
    height = stack.shape[1]
    breadth = stack.shape[2]
    return (
        stack.reshape(grid_rows, grid_cols, height, breadth)
        .transpose(0, 2, 1, 3)
        .reshape(grid_rows * height, grid_cols * breadth)
    )


def disassemble(whole, grid_rows, grid_cols):
    height = whole.shape[0] // grid_rows
    breadth = whole.shape[1] // grid_cols
    return (
        whole.reshape(grid_rows, height, grid_cols, breadth)
        .transpose(0, 2, 1, 3)
        .reshape(grid_rows * grid_cols, height, breadth)
    )


def fetch_attention(
    query_weight, key_weight, value_weight, output_weight, first_gain, grid_rows, grid_cols
):
    pieces = (
        lax.all_gather(query_weight[None], ("row", "col"), axis=0, tiled=True),
        lax.all_gather(key_weight[None], ("row", "col"), axis=0, tiled=True),
        lax.all_gather(value_weight[None], ("row", "col"), axis=0, tiled=True),
        lax.all_gather(output_weight[None], ("row", "col"), axis=0, tiled=True),
        lax.all_gather(first_gain[None], ("row", "col"), axis=0, tiled=True),
    )
    wholes = tuple((assemble(piece, grid_rows, grid_cols) for piece in pieces[:4]))
    return wholes + (pieces[4].reshape(-1).astype(jnp.float32),)


def fetch_feedforward(gate_weight, up_weight, down_weight, second_gain, grid_rows, grid_cols):
    pieces = (
        lax.all_gather(gate_weight[None], ("row", "col"), axis=0, tiled=True),
        lax.all_gather(up_weight[None], ("row", "col"), axis=0, tiled=True),
        lax.all_gather(down_weight[None], ("row", "col"), axis=0, tiled=True),
        lax.all_gather(second_gain[None], ("row", "col"), axis=0, tiled=True),
    )
    wholes = tuple((assemble(piece, grid_rows, grid_cols) for piece in pieces[:3]))
    return wholes + (pieces[3].reshape(-1).astype(jnp.float32),)


def rms_scale(values):
    return lax.rsqrt(jnp.mean(values * values, axis=-1, keepdims=True) + EPSILON)


def rotate(values, cosine, sine):
    half = values.shape[-1] // 2
    front = values[..., :half]
    behind = values[..., half:]
    return jnp.concatenate(
        [front * cosine - behind * sine, behind * cosine + front * sine], axis=-1
    )


def split_heads(values, head_count):
    return values.reshape(values.shape[0], head_count, -1).transpose(1, 0, 2)


def join_heads(values):
    return values.transpose(1, 0, 2).reshape(values.shape[1], -1)


def attend_head(operands, allowed, score_scale):
    queries, keys, values = operands
    scores = jnp.einsum("qd,kd->qk", queries, keys, preferred_element_type=jnp.float32)
    logits = jnp.where(allowed, scores * score_scale, NEGATIVE)
    row_top = jnp.max(logits, axis=1, keepdims=True)
    weights = jnp.exp(logits - row_top)
    row_total = jnp.sum(weights, axis=1, keepdims=True)
    probs_low = (weights / row_total).astype(jnp.bfloat16)
    context = jnp.dot(probs_low, values, preferred_element_type=jnp.float32)
    return (context, row_top[:, 0], row_total[:, 0])


def attend_back(operands, allowed, score_scale):
    queries, keys, values, row_top, row_total, grad_context = operands
    scores = jnp.einsum("qd,kd->qk", queries, keys, preferred_element_type=jnp.float32)
    logits = jnp.where(allowed, scores * score_scale, NEGATIVE)
    probs = jnp.exp(logits - row_top[:, None]) / row_total[:, None]
    probs_low = probs.astype(jnp.bfloat16)
    grad_vals = jnp.einsum("qk,qd->kd", probs_low, grad_context, preferred_element_type=jnp.float32)
    grad_probs = jnp.einsum("qd,kd->qk", grad_context, values, preferred_element_type=jnp.float32)
    inner = jnp.sum(probs * grad_probs, axis=1, keepdims=True)
    grad_scores = (jnp.where(allowed, probs * (grad_probs - inner), 0.0) * score_scale).astype(
        jnp.bfloat16
    )
    grad_qrot = jnp.dot(grad_scores, keys, preferred_element_type=jnp.float32)
    grad_krot = jnp.einsum("qk,qd->kd", grad_scores, queries, preferred_element_type=jnp.float32)
    return (grad_qrot, grad_krot, grad_vals)


def weight_term(left, right):
    return jnp.einsum("ta,tb->ab", left, right, preferred_element_type=jnp.float32)


def back_product(grad, weight):
    return jnp.einsum("tb,ab->ta", grad, weight, preferred_element_type=jnp.float32)


def on_device(
    inputs,
    segment_ids,
    query_weight,
    key_weight,
    value_weight,
    output_weight,
    gate_weight,
    up_weight,
    down_weight,
    first_gain,
    second_gain,
    cotangent,
):
    grid_rows = lax.axis_size("row")
    grid_cols = lax.axis_size("col")
    token_count, model_width = inputs.shape
    head_count = model_width // HEAD_DIM
    score_scale = HEAD_DIM ** (-0.5)
    token_index = jnp.arange(token_count, dtype=jnp.int32)
    same_seq = segment_ids[:, None] == segment_ids[None, :]
    allowed = same_seq & (token_index[None, :] <= token_index[:, None])
    starts = jnp.min(jnp.where(same_seq, token_index[None, :], token_count), axis=1)
    positions = (token_index - starts).astype(jnp.float32)
    frequencies = ROPE_BASE ** (-2.0 * jnp.arange(HEAD_DIM // 2, dtype=jnp.float32) / HEAD_DIM)
    phases = positions[:, None] * frequencies[None, :]
    cosine = jnp.cos(phases)[:, None, :]
    sine = jnp.sin(phases)[:, None, :]
    w_query, w_key, w_value, w_output, gain_one = fetch_attention(
        query_weight, key_weight, value_weight, output_weight, first_gain, grid_rows, grid_cols
    )
    query_flat = jnp.dot(inputs, w_query, preferred_element_type=jnp.float32)
    key_flat = jnp.dot(inputs, w_key, preferred_element_type=jnp.float32)
    value_flat = jnp.dot(inputs, w_value, preferred_element_type=jnp.float32)
    queries = rotate(query_flat.reshape(token_count, head_count, HEAD_DIM), cosine, sine).astype(
        jnp.bfloat16
    )
    keys = rotate(key_flat.reshape(token_count, head_count, HEAD_DIM), cosine, sine).astype(
        jnp.bfloat16
    )
    query_heads = queries.transpose(1, 0, 2)
    key_heads = keys.transpose(1, 0, 2)
    value_heads = split_heads(value_flat.astype(jnp.bfloat16), head_count)

    def head_forward(operands):
        return attend_head(operands, allowed, score_scale)

    contexts, row_tops, row_totals = lax.map(head_forward, (query_heads, key_heads, value_heads))
    context = join_heads(contexts).astype(jnp.bfloat16)
    first_sum = inputs.astype(jnp.float32) + jnp.dot(
        context, w_output, preferred_element_type=jnp.float32
    )
    scale_one = rms_scale(first_sum)
    normed_one = first_sum * scale_one
    normed = normed_one * gain_one
    hidden_in = normed.astype(jnp.bfloat16)
    w_gate, w_up, w_down, gain_two = fetch_feedforward(
        gate_weight, up_weight, down_weight, second_gain, grid_rows, grid_cols
    )
    gate_act = jnp.dot(hidden_in, w_gate, preferred_element_type=jnp.float32)
    up_act = jnp.dot(hidden_in, w_up, preferred_element_type=jnp.float32)
    gate_sigmoid = jax.nn.sigmoid(gate_act)
    hidden = (gate_act * gate_sigmoid * up_act).astype(jnp.bfloat16)
    second_sum = normed + jnp.dot(hidden, w_down, preferred_element_type=jnp.float32)
    scale_two = rms_scale(second_sum)
    normed_two = second_sum * scale_two
    layer_out = (normed_two * gain_two).astype(jnp.bfloat16)
    grad_out = cotangent.astype(jnp.float32)
    gain_two_term = jnp.sum(grad_out * normed_two, axis=0)
    grad_norm_two = grad_out * gain_two
    grad_second = scale_two * (
        grad_norm_two - normed_two * jnp.mean(grad_norm_two * normed_two, axis=-1, keepdims=True)
    )
    grad_branch_two = grad_second.astype(jnp.bfloat16)
    w_gate, w_up, w_down, gain_two = fetch_feedforward(
        gate_weight, up_weight, down_weight, second_gain, grid_rows, grid_cols
    )
    down_term = weight_term(hidden, grad_branch_two)
    grad_hidden = back_product(grad_branch_two, w_down)
    grad_gate = (
        grad_hidden * up_act * (gate_sigmoid + gate_act * gate_sigmoid * (1.0 - gate_sigmoid))
    ).astype(jnp.bfloat16)
    grad_up = (grad_hidden * gate_act * gate_sigmoid).astype(jnp.bfloat16)
    gate_term = weight_term(hidden_in, grad_gate)
    up_term = weight_term(hidden_in, grad_up)
    grad_normed = grad_second + back_product(grad_gate, w_gate) + back_product(grad_up, w_up)
    gain_lanes = gain_two_term.reshape(grid_rows * grid_cols, -1)
    feed_shares = (
        lax.psum_scatter(
            disassemble(gate_term, grid_rows, grid_cols),
            ("row", "col"),
            scatter_dimension=0,
            tiled=True,
        ),
        lax.psum_scatter(
            disassemble(up_term, grid_rows, grid_cols),
            ("row", "col"),
            scatter_dimension=0,
            tiled=True,
        ),
        lax.psum_scatter(
            disassemble(down_term, grid_rows, grid_cols),
            ("row", "col"),
            scatter_dimension=0,
            tiled=True,
        ),
        lax.psum_scatter(gain_lanes, ("row", "col"), scatter_dimension=0, tiled=True),
    )
    gain_one_term = jnp.sum(grad_normed * normed_one, axis=0)
    grad_norm_one = grad_normed * gain_one
    grad_first = scale_one * (
        grad_norm_one - normed_one * jnp.mean(grad_norm_one * normed_one, axis=-1, keepdims=True)
    )
    grad_branch_one = grad_first.astype(jnp.bfloat16)
    w_query, w_key, w_value, w_output, gain_one = fetch_attention(
        query_weight, key_weight, value_weight, output_weight, first_gain, grid_rows, grid_cols
    )
    output_term = weight_term(context, grad_branch_one)
    grad_context = back_product(grad_branch_one, w_output).astype(jnp.bfloat16)

    def head_backward(operands):
        return attend_back(operands, allowed, score_scale)

    grad_qrots, grad_krots, grad_valss = lax.map(
        head_backward,
        (
            query_heads,
            key_heads,
            value_heads,
            row_tops,
            row_totals,
            split_heads(grad_context, head_count),
        ),
    )
    grad_query = (
        rotate(grad_qrots.transpose(1, 0, 2), cosine, -sine)
        .reshape(token_count, model_width)
        .astype(jnp.bfloat16)
    )
    grad_key = (
        rotate(grad_krots.transpose(1, 0, 2), cosine, -sine)
        .reshape(token_count, model_width)
        .astype(jnp.bfloat16)
    )
    grad_value = join_heads(grad_valss).astype(jnp.bfloat16)
    query_term = weight_term(inputs, grad_query)
    key_term = weight_term(inputs, grad_key)
    value_term = weight_term(inputs, grad_value)
    input_grad = (
        grad_first
        + back_product(grad_query, w_query)
        + back_product(grad_key, w_key)
        + back_product(grad_value, w_value)
    ).astype(jnp.bfloat16)
    attention_parts = (
        disassemble(query_term, grid_rows, grid_cols),
        disassemble(key_term, grid_rows, grid_cols),
        disassemble(value_term, grid_rows, grid_cols),
        disassemble(output_term, grid_rows, grid_cols),
    )
    first_lanes = gain_one_term.reshape(grid_rows * grid_cols, -1)
    attention_shares = lax.psum_scatter(
        attention_parts + (first_lanes,), ("row", "col"), scatter_dimension=0, tiled=True
    )
    shares = attention_shares[:4] + feed_shares[:3] + (attention_shares[4], feed_shares[3])
    summed = jax.tree.map(
        lambda part: part.astype(jnp.float32),
        lax.psum(for_sending(tuple((share[0] for share in shares))), "dp"),
    )
    return (
        layer_out,
        input_grad,
        summed[0],
        summed[1],
        summed[2],
        summed[3],
        summed[4],
        summed[5],
        summed[6],
        summed[7],
        summed[8],
    )


def solution(mesh):
    placed = (
        P(("dp", "row", "col"), None),
        P(("dp", "row", "col")),
        P("row", "col"),
        P("row", "col"),
        P("row", "col"),
        P("row", "col"),
        P("row", "col"),
        P("row", "col"),
        P("row", "col"),
        P(("row", "col")),
        P(("row", "col")),
        P(("dp", "row", "col"), None),
    )
    return jax.shard_map(
        on_device,
        mesh=mesh,
        in_specs=placed,
        out_specs=(
            P(("dp", "row", "col"), None),
            P(("dp", "row", "col"), None),
            P("row", "col"),
            P("row", "col"),
            P("row", "col"),
            P("row", "col"),
            P("row", "col"),
            P("row", "col"),
            P("row", "col"),
            P(("row", "col")),
            P(("row", "col")),
        ),
        check_vma=False,
    )
```

profile of v0, /device:TPU:0, one launch (start us, length us, event | category | flops | bytes accessed | tf_op | source)
XLA Modules:
  0.0 1591.9 jit_solution(5571109859749134416)
XLA Ops:
  18.3 44.6 %all-reduce.5 = (bf16[768]{0:T(1024)(128)(2,1)S(1)}, bf16[768]{0:T(1024)(128)(2,1)S(1)}) all-reduce(bf16[768]{0:T(1024)(128)(2,1)S(1)} %dynamic-update-slice, bf16[768]{0:T(1024)(128)(2,1)S(1)} %dynamic-update-slice.1), channel_id=6, replica_groups=mesh['dp'=2,'row'=4,'col'=4] {'row','col'}, use_global_device_ids=true, to_apply=%add | all-reduce | flops 1536 | bytes 6144
  65.8 5.8 all-gather.19.cloned.1.call-done
  76.7 4.4 fusion.54
  81.2 50.0 %all-gather.17.cloned.1.call-done = bf16[3072,192]{1,0:T(8,128)(2,1)} async-done(((bf16[192,192]{1,0:T(8,128)(2,1)}), bf16[3072,192]{1,0:T(8,128)(2,1)}) %all-gather.17.cloned.1.call-update) | async-done | bytes 1179664 | tf_op jit(solution)/shard_map/all_gather | solution.py:44
  146.2 44.5 %all-gather.21.cloned.1.call-done = bf16[3072,192]{1,0:T(8,128)(2,1)} async-done(((bf16[192,192]{1,0:T(8,128)(2,1)}), bf16[3072,192]{1,0:T(8,128)(2,1)}) %all-gather.21.cloned.1.call-update) | async-done | bytes 1179664 | tf_op jit(solution)/shard_map/all_gather | solution.py:46
  194.7 4.4 convolution_convert_fusion.1
  199.2 4.3 copy.128
  203.5 56.9 %while.32 = (s32[]{:T(128)}, bf16[12,1024,64]{1,2,0:T(8,128)(2,1)S(1)}, f32[12,1024]{1,0:T(8,128)S(1)}, f32[12,1024]{1,0:T(8,128)S(1)}, bf16[12,1024,64]{2,1,0:T...) while((s32[]{:T(128)}, ...), condition=%wide.region_4.5_spmd.clone.clone, body=%wide.region_1.4_spmd.clone.sunk.clone | while | flops 279967744 | bytes 13678685 | solution.py:170
  260.4 3.2 copy.161
  265.8 3.8 multiply_reduce_fusion.4
  271.4 48.1 %all-gather.25.cloned.1.call-done = bf16[3072,512]{1,0:T(8,128)(2,1)} async-done(((bf16[192,512]{1,0:T(8,128)(2,1)}), bf16[3072,512]{1,0:T(8,128)(2,1)}) %all-gather.25.cloned.1.call-update) | async-done | bytes 3145744 | tf_op jit(solution)/shard_map/all_gather | solution.py:56
  319.5 4.3 copy.132
  326.6 62.2 %all-gather.27.cloned.1.call-done = bf16[3072,512]{1,0:T(8,128)(2,1)} async-done(((bf16[192,512]{1,0:T(8,128)(2,1)}), bf16[3072,512]{1,0:T(8,128)(2,1)}) %all-gather.27.cloned.1.call-update) | async-done | bytes 3145744 | tf_op jit(solution)/shard_map/all_gather | solution.py:57
  388.8 4.3 copy.133
  395.7 65.5 %all-gather.29.cloned.1.call-done = bf16[8192,192]{0,1:T(8,128)(2,1)} async-done(((bf16[512,192]{0,1:T(8,128)(2,1)}), bf16[8192,192]{0,1:T(8,128)(2,1)}) %all-gather.29.cloned.1.call-update) | async-done | bytes 3145744 | tf_op jit(solution)/shard_map/all_gather | solution.py:58
  461.2 6.6 reshape.314
  467.8 3.1 copy.134
  473.2 3.6 fusion.73
  476.9 7.8 multiply_convert_fusion.3
  484.6 5.7 multiply_reduce_fusion.3
  493.2 12.6 multiply_convert_fusion.1
  505.8 5.5 fusion.74
  511.4 4.6 multiply_reduce_fusion.1
  520.7 3.5 fusion.77
  525.6 2.9 copy.136
  528.5 155.0 %while.33 = (s32[]{:T(128)}, f32[12,1024,64]{1,2,0:T(8,128)}, f32[12,1024,64]{1,2,0:T(8,128)}, bf16[12,1024,64]{1,2,0:T(8,128)(2,1)S(1)}, bf16[12,1024,64]{2,1,0...) while((s32[]{:T(128)}, f32[12,1024,64]{1,2,0:T(8,128)}, ...), condition=%wide.region_11.12_spmd.clone.clone, body=%wide.region_9.11_spmd.clone.sunk.clone | while | flops 689961984 | bytes 34129008 | solution.py:246
  530.3 3.3 multiply_reduce_fusion.7
  543.3 3.2 multiply_reduce_fusion.7
  556.2 3.3 multiply_reduce_fusion.7
  569.1 3.3 multiply_reduce_fusion.7
  582.1 3.3 multiply_reduce_fusion.7
  595.0 3.2 multiply_reduce_fusion.7
  607.9 3.3 multiply_reduce_fusion.7
  620.8 3.3 multiply_reduce_fusion.7
  633.7 3.3 multiply_reduce_fusion.7
  646.6 3.2 multiply_reduce_fusion.7
  659.5 3.3 multiply_reduce_fusion.7
  672.4 3.3 multiply_reduce_fusion.7
  683.6 4.4 multiply_subtract_fusion.1
  692.7 4.9 reshape.317
  697.7 4.8 copy.142
  707.4 4.9 reshape.319
  712.3 4.7 copy.143
  721.2 3.7 reshape.321
  724.9 2.9 copy.144
  729.2 9.4 fusion.58
  738.6 8.5 reshape.328
  747.0 7.4 copy.148
  755.9 7.4 fusion.79
  763.3 8.4 reshape.326
  771.7 7.3 copy.146
  779.1 7.5 fusion.78
  786.6 8.4 reshape.324
  795.0 7.7 copy.145
  803.5 74.5 %all-reduce.4 = (bf16[16,48]{1,0:T(8,128)(2,1)S(1)}, bf16[16,48]{1,0:T(8,128)(2,1)S(1)}) all-reduce(f32[16,48]{1,0:T(8,128)S(1)} %reshape.330, f32[16,48]{1,0:T(8,128)S(1)} %reshape.331), channel_id=18, replica_groups=mesh['dp'=2,'row'=4,'col'=4] {'row','col'}, use_global_device_ids=true, to_apply=%region_27.28.clone | all-reduce | flops 1536 | bytes 9216
  878.7 3.2 fusion.75
  881.9 3.2 fusion.76
  888.4 77.9 %reduce-scatter.10.cloned.1.call-done = f32[1,192,192]{2,1,0:T(8,128)} async-done(((f32[16,192,192]{2,1,0:T(8,128)}), f32[1,192,192]{2,1,0:T(8,128)}) %reduce-scatter.10.cloned.1.call-update) | async-done | bytes 147472 | tf_op jit(solution)/shard_map/reduce_scatter | solution.py:284
  967.9 133.2 %reduce-scatter.12.cloned.1.call-done = f32[1,192,192]{2,1,0:T(8,128)} async-done(((f32[16,192,192]{2,1,0:T(8,128)}), f32[1,192,192]{2,1,0:T(8,128)}) %reduce-scatter.12.cloned.1.call-update) | async-done | bytes 147472 | tf_op jit(solution)/shard_map/reduce_scatter | solution.py:284
  1102.7 148.1 %reduce-scatter.20.cloned.1.call-done = f32[1,512,192]{1,2,0:T(8,128)} async-done(((f32[16,512,192]{1,2,0:T(8,128)}), f32[1,512,192]{1,2,0:T(8,128)}) %reduce-scatter.20.cloned.1.call-update) | async-done | bytes 393232 | tf_op jit(solution)/shard_map/reduce_scatter | solution.py:223
  1252.5 148.5 %reduce-scatter.18.cloned.1.call-done = f32[1,192,512]{2,1,0:T(8,128)} async-done(((f32[16,192,512]{2,1,0:T(8,128)}), f32[1,192,512]{2,1,0:T(8,128)}) %reduce-scatter.18.cloned.1.call-update) | async-done | bytes 393232 | tf_op jit(solution)/shard_map/reduce_scatter | solution.py:217
  1402.7 148.1 %reduce-scatter.16.cloned.1.call-done = f32[1,192,512]{2,1,0:T(8,128)} async-done(((f32[16,192,512]{2,1,0:T(8,128)}), f32[1,192,512]{2,1,0:T(8,128)}) %reduce-scatter.16.cloned.1.call-update) | async-done | bytes 393232 | tf_op jit(solution)/shard_map/reduce_scatter | solution.py:211
  1556.9 7.9 add_convert_fusion
  1569.0 4.7 all-reduce.10.cloned.1.call-done
  (334 shorter events, 279.5 us)
Async XLA Ops:
  7.2 64.4 %all-gather.19.cloned.1.call-start = ((), (), s32[]{:S(2)}) async-start(), calls=%async_computation.15 | async-start | bytes 1671168 | tf_op jit(solution)/shard_map/all_gather | solution.py:45
  7.9 123.2 %all-gather.17.cloned.1.call-start = ((), (), s32[]{:S(2)}) async-start(), calls=%async_computation.14 | async-start | bytes 1671168 | tf_op jit(solution)/shard_map/all_gather | solution.py:44
  8.7 182.0 %all-gather.21.cloned.1.call-start = ((), (), s32[]{:S(2)}) async-start(), calls=%async_computation.16 | async-start | bytes 1671168 | tf_op jit(solution)/shard_map/all_gather | solution.py:46
  9.4 251.0 %all-gather.23.cloned.1.call-start = ((), (), s32[]{:S(2)}) async-start(), calls=%async_computation.17 | async-start | bytes 1671168 | tf_op jit(solution)/shard_map/all_gather | solution.py:47
  10.0 309.6 %all-gather.25.cloned.1.call-start = ((), (), s32[]{:S(2)}) async-start(), calls=%async_computation.18 | async-start | bytes 3342336 | tf_op jit(solution)/shard_map/all_gather | solution.py:56
  10.6 378.2 %all-gather.27.cloned.1.call-start = ((), (), s32[]{:S(2)}) async-start(), calls=%async_computation.19 | async-start | bytes 3342336 | tf_op jit(solution)/shard_map/all_gather | solution.py:57
  11.1 450.1 %all-gather.29.cloned.1.call-start = ((), (), s32[]{:S(2)}) async-start(), calls=%async_computation.20 | async-start | bytes 3342336 | tf_op jit(solution)/shard_map/all_gather | solution.py:58
  11.9 873.2 %reduce-scatter.14.cloned.1.call-start = ((), (), s32[]{:S(2)}) async-start(), calls=%async_computation.10 | async-start | bytes 3342336 | tf_op jit(solution)/shard_map/reduce_scatter | solution.py:284
  12.1 4.4 copy-start.2
  13.8 2.8 copy-start.45
  13.8 4.1 copy-start.46
  13.8 4.3 copy-start.47
  13.8 49.1 %copy-start.17 = (bf16[1024,768]{1,0:T(8,128)(2,1)S(1)}, bf16[1024,768]{1,0:T(8,128)(2,1)}, u32[]{:S(2)}) copy-start(bf16[1024,768]{1,0:T(8,128)(2,1)} %param.27) | copy-start | bytes 4718596
  62.9 453.1 %copy-start.36 = (f32[768]{0:T(1024)}, f32[768]{0:T(1024)S(1)}, u32[]{:S(2)}) copy-start(f32[768]{0:T(1024)S(1)} %convert_element_type.259) | copy-start | bytes 9220
  64.6 12.1 copy-start.18
  65.8 73.3 %copy-start.29 = (f32[1024,32]{0,1:T(8,128)}, f32[1024,32]{0,1:T(8,128)S(1)}, u32[]{:S(2)}) copy-start(f32[1024,32]{0,1:T(8,128)S(1)} %get-tuple-element.394) | copy-start | bytes 393220
  136.3 2.8 copy-start.16
  194.7 4.4 copy-start.12
  199.2 4.3 copy-start.7
  199.2 4.3 copy-start.34
  260.3 5.5 copy-start.5
  269.6 246.4 %copy-start = (f32[1024,768]{0,1:T(8,128)}, f32[1024,768]{0,1:T(8,128)S(1)}, u32[]{:S(2)}) copy-start(f32[1024,768]{0,1:T(8,128)S(1)} %get-tuple-element.398) | copy-start | bytes 9437188
  269.6 246.4 %copy-start.38 = (f32[1024]{0:T(1024)}, f32[1024]{0:T(1024)S(1)}, u32[]{:S(2)}) copy-start(f32[1024]{0:T(1024)S(1)} %add_rsqrt_fusion.1) | copy-start | bytes 12292
  470.9 1.9 copy-start.14
  470.9 2.3 copy-start.26
  473.2 3.6 copy-start.15
  476.8 7.8 copy-start.48
  484.6 5.7 copy-start.9
  490.3 21.1 %copy-start.13 = (f32[1024,768]{0,1:T(8,128)}, f32[1024,768]{0,1:T(8,128)S(1)}, u32[]{:S(2)}) copy-start(f32[1024,768]{0,1:T(8,128)S(1)} %get-tuple-element.402) | copy-start | bytes 9437188
  493.2 18.2 %copy-start.43 = (f32[1024]{0:T(1024)}, f32[1024]{0:T(1024)S(1)}, u32[]{:S(2)}) copy-start(f32[1024]{0:T(1024)S(1)} %broadcast_multiply_fusion.1) | copy-start | bytes 12292
  505.8 5.6 copy-start.49
  516.0 1.6 copy-start.8
  516.0 1.6 copy-start.40
  516.0 2.2 copy-start.33
  518.2 2.5 copy-start.6
  524.2 1.4 copy-start.28
  524.2 4.3 copy-start.3
  524.2 362.6 %reduce-scatter.8.cloned.1.call-start = ((), (), s32[]{:S(2)}) async-start(), calls=%async_computation.7 | async-start | bytes 3342336 | tf_op jit(solution)/shard_map/reduce_scatter | solution.py:284
  528.5 155.0 %copy-start.30 = (f32[1024,32]{0,1:T(8,128)S(1)}, f32[1024,32]{0,1:T(8,128)}, u32[]{:S(2)}) copy-start(f32[1024,32]{0,1:T(8,128)} %copy-done.29) | copy-start | bytes 393220
  528.5 155.0 %copy-start.35 = (f32[1024,32]{0,1:T(8,128)S(1)}, f32[1024,32]{0,1:T(8,128)}, u32[]{:S(2)}) copy-start(f32[1024,32]{0,1:T(8,128)} %get-tuple-element.392) | copy-start | bytes 393220
  683.6 33.9 %copy-start.4 = (bf16[12,1024,64]{1,2,0:T(8,128)(2,1)}, bf16[12,1024,64]{1,2,0:T(8,128)(2,1)S(1)}, u32[]{:S(2)}) copy-start(bf16[12,1024,64]{1,2,0:T(8,128)(2,1)S(1)} %get-tuple-element.119) | copy-start | bytes 4718596
  688.0 2.0 copy-start.19
  688.2 1.2 copy-start.22
  702.5 263.8 %reduce-scatter.10.cloned.1.call-start = ((), (), s32[]{:S(2)}) async-start(), calls=%async_computation.8 | async-start | bytes 3342336 | tf_op jit(solution)/shard_map/reduce_scatter | solution.py:284
  702.6 2.0 copy-start.20
  702.7 1.1 copy-start.24
  717.0 1.4 copy-start.21
  717.0 384.1 %reduce-scatter.12.cloned.1.call-start = ((), (), s32[]{:S(2)}) async-start(), calls=%async_computation.9 | async-start | bytes 3342336 | tf_op jit(solution)/shard_map/reduce_scatter | solution.py:284
  727.8 1.4 copy-start.10
  727.8 1.4 copy-start.44
  727.8 523.0 %reduce-scatter.20.cloned.1.call-start = ((), (), s32[]{:S(2)}) async-start(), calls=%async_computation.13 | async-start | bytes 6684672 | tf_op jit(solution)/shard_map/reduce_scatter | solution.py:223
  754.5 1.4 copy-start.27
  754.5 646.5 %reduce-scatter.18.cloned.1.call-start = ((), (), s32[]{:S(2)}) async-start(), calls=%async_computation.12 | async-start | bytes 6684672 | tf_op jit(solution)/shard_map/reduce_scatter | solution.py:217
  779.1 771.7 %reduce-scatter.16.cloned.1.call-start = ((), (), s32[]{:S(2)}) async-start(), calls=%async_computation.11 | async-start | bytes 6684672 | tf_op jit(solution)/shard_map/reduce_scatter | solution.py:211
  802.7 75.9 %copy-start.23 = (bf16[1024,12,64]{0,2,1:T(8,128)(2,1)S(1)}, bf16[1024,12,64]{0,2,1:T(8,128)(2,1)}, u32[]{:S(2)}) copy-start(bf16[1024,12,64]{0,2,1:T(8,128)(2,1)} %copy-done.22) | copy-start | bytes 4718596
  802.7 75.9 %copy-start.32 = (bf16[768,768]{0,1:T(8,128)(2,1)S(1)}, bf16[768,768]{0,1:T(8,128)(2,1)}, u32[]{:S(2)}) copy-start(bf16[768,768]{0,1:T(8,128)(2,1)} %reshape.302) | copy-start | bytes 3538948
  802.7 771.0 %all-reduce.10.cloned.1.call-start = ((), (), s32[]{:S(2)}) async-start(), calls=%async_computation.21 | async-start | bytes 1966080 | tf_op jit(solution)/shard_map/psum | solution.py:290
  878.7 3.2 copy-start.25
  878.7 3.2 copy-start.31
  885.1 671.8 %copy-start.1 = (f32[1024,768]{0,1:T(8,128)S(1)}, f32[1024,768]{0,1:T(8,128)}, u32[]{:S(2)}) copy-start(f32[1024,768]{0,1:T(8,128)} %copy-done) | copy-start | bytes 9437188
  885.1 671.8 %copy-start.37 = (f32[768]{0:T(1024)S(1)}, f32[768]{0:T(1024)}, u32[]{:S(2)}) copy-start(f32[768]{0:T(1024)} %copy-done.36) | copy-start | bytes 9220
  885.1 671.8 %copy-start.39 = (f32[1024]{0:T(1024)S(1)}, f32[1024]{0:T(1024)}, u32[]{:S(2)}) copy-start(f32[1024]{0:T(1024)} %copy-done.38) | copy-start | bytes 12292
  885.1 671.8 %copy-start.41 = (f32[1024]{0:T(1024)S(1)}, f32[1024]{0:T(1024)}, u32[]{:S(2)}) copy-start(f32[1024]{0:T(1024)} %copy-done.40) | copy-start | bytes 12292
  1564.8 2.7 copy-start.11
  (1 other events, 0.7 us)
Sparse Core Ops, SparseCore 0:
  10.9 60.7 all-gather.18
  74.4 56.6 all-gather.16
  134.0 56.6 all-gather.20
  193.4 56.6 all-gather.22
  252.7 66.7 all-gather.24
  322.2 66.5 all-gather.26
  391.5 69.6 all-gather.28
  524.4 128.8 reduce-scatter.13
  702.6 128.9 reduce-scatter.7
  836.5 129.8 reduce-scatter.9
  971.3 129.7 reduce-scatter.11
  1106.2 144.5 reduce-scatter.19
  1256.0 144.9 reduce-scatter.17
  1406.1 144.6 reduce-scatter.15
  1554.6 19.0 all-reduce.9
where the time goes:
time: 1600 us; the launch traced here: 1590 us
  waiting for transfers between devices  941 us (59%)
  matrix products  290 us (18%)
  local copies, waits for them, and re-layouts  157 us (10%)
  blocking collectives  122 us (8%)
  other arithmetic  64.3 us (4%)
    reduce_scatter x4, waiting for transfers between devices, on_device(): lax.psum_scatter(attention_parts + (first_lanes,), ('row', 'col'), scatte...  211 us
    reduce_scatter x1, waiting for transfers between devices, on_device(): lax.psum_scatter(disassemble(up_term, grid_rows, grid_cols), ('row', 'col...  148 us
    reduce_scatter x1, waiting for transfers between devices, on_device(): lax.psum_scatter(disassemble(down_term, grid_rows, grid_cols), ('row', 'c...  148 us
    reduce_scatter x1, waiting for transfers between devices, on_device(): lax.psum_scatter(disassemble(gate_term, grid_rows, grid_cols), ('row', 'c...  148 us
    unnamed x2, blocking collectives  119 us
    all_gather x1, waiting for transfers between devices, fetch_feedforward(): lax.all_gather(down_weight[None], ('row', 'col'), axis=0, tiled=True)  65.5 us
    all_gather x1, waiting for transfers between devices, fetch_feedforward(): lax.all_gather(up_weight[None], ('row', 'col'), axis=0, tiled=True)  62.2 us
    all_gather x1, waiting for transfers between devices, fetch_attention(): lax.all_gather(query_weight[None], ('row', 'col'), axis=0, tiled=True)  50 us
  transfers between devices with their start and end apart: 15, of which 12 were waited for; matrix products, arithmetic and copies ran while one was open for 27% of the time, Pallas kernels for 0%

commit v1 on v0

--- a/solution.py
+++ b/solution.py
@@ -7,6 +7,33 @@
 EPSILON = 1e-06
 ROPE_BASE = 10000.0
 NEGATIVE = -1e30
+
+
+def number_the_sides(vals, lane_axis):
+    formed = lax.axis_size(lane_axis)
+    part_now = lax.axis_index(lane_axis)
+    block_out, arr_out, latest = (formed, part_now, vals.shape[0])
+    block_next = range(block_out)
+    spare = map(lambda p: (p, (p + 1) % block_out), block_next)
+    log = list(spare)
+    item_now = range(block_out)
+    mat_out = map(lambda p: (p, (p - 1) % block_out), item_now)
+    panels = list(mat_out)
+    a_next = jnp.zeros((*vals.shape[:0], block_out * latest, *vals.shape[1:]), vals.dtype)
+    a_next = lax.dynamic_update_slice_in_dim(a_next, vals, arr_out * latest, axis=0)
+    work_now = later = vals
+    piece_now = block_out // 2
+    for dev_j in range(1, piece_now + 1):
+        work_now = lax.ppermute(work_now, lane_axis, log)
+        a_next = lax.dynamic_update_slice_in_dim(
+            a_next, work_now, (arr_out - dev_j) % block_out * latest, axis=0
+        )
+        if dev_j < block_out - piece_now:
+            later = lax.ppermute(later, lane_axis, panels)
+            a_next = lax.dynamic_update_slice_in_dim(
+                a_next, later, (arr_out + dev_j) % block_out * latest, axis=0
+            )
+    return a_next
 
 
 def for_sending(value):
@@ -54,7 +81,7 @@
 def fetch_feedforward(gate_weight, up_weight, down_weight, second_gain, grid_rows, grid_cols):
     pieces = (
         lax.all_gather(gate_weight[None], ("row", "col"), axis=0, tiled=True),
-        lax.all_gather(up_weight[None], ("row", "col"), axis=0, tiled=True),
+        number_the_sides(up_weight[None], ("row", "col")),
         lax.all_gather(down_weight[None], ("row", "col"), axis=0, tiled=True),
         lax.all_gather(second_gain[None], ("row", "col"), axis=0, tiled=True),
     )

time: 1600 us -> 1550 us (0.969)
  waiting for transfers between devices: 941 us -> 855 us
  starting transfers between devices: 1.17 us -> 36.7 us
    all_gather x1 -> x0, waiting for transfers between devices: 62.2 us -> none  [fetch_feedforward(): lax.all_gather(up_weight[None], ('row', 'col'), axis=0, tiled=True)]
    all_gather x1, waiting for transfers between devices: 50 us -> 0.01 us  [fetch_attention(): lax.all_gather(query_weight[None], ('row', 'col'), axis=0, tiled=True)]
    ppermute x0 -> x15, waiting for transfers between devices: none -> 45.1 us  [the longest x8 24 us: number_the_sides(): work_now = lax.ppermute(work_now, lane_axis, log)]
    ppermute x0 -> x15, starting transfers between devices: none -> 35.5 us  [the longest x7 24.3 us: number_the_sides(): later = lax.ppermute(later, lane_axis, panels)]
    unnamed x114 -> x116, local copies, waits for them, and re-layouts: 33.5 us -> 33.6 us
  transfers between devices with their start and end apart: 15 -> 29, of which waited for: 12 -> 21; matrix products, arithmetic and copies ran while one was open for 27% -> 28% of each run, Pallas kernels for 0% -> 0%
where the time goes in v1:
time: 1550 us; the launch traced here: 1540 us
  waiting for transfers between devices  855 us (55%)
  matrix products  291 us (19%)
  local copies, waits for them, and re-layouts  158 us (10%)
  blocking collectives  116 us (7%)
  other arithmetic  64.3 us (4%)
  starting transfers between devices  36.7 us (2%)
  between operations  15.9 us (1%)
    reduce_scatter x4, waiting for transfers between devices, on_device(): lax.psum_scatter(attention_parts + (first_lanes,), ('row', 'col'), scatte...  211 us
    reduce_scatter x1, waiting for transfers between devices, on_device(): lax.psum_scatter(disassemble(down_term, grid_rows, grid_cols), ('row', 'c...  149 us
    reduce_scatter x1, waiting for transfers between devices, on_device(): lax.psum_scatter(disassemble(gate_term, grid_rows, grid_cols), ('row', 'c...  149 us
    reduce_scatter x1, waiting for transfers between devices, on_device(): lax.psum_scatter(disassemble(up_term, grid_rows, grid_cols), ('row', 'col...  148 us
    unnamed x2, blocking collectives  113 us
    all_gather x1, waiting for transfers between devices, fetch_feedforward(): lax.all_gather(down_weight[None], ('row', 'col'), axis=0, tiled=True)  65.3 us
    all_gather x1, waiting for transfers between devices, fetch_feedforward(): lax.all_gather(gate_weight[None], ('row', 'col'), axis=0, tiled=True)  48 us
    dot_general x7, matrix products, back_product(): jnp.einsum('tb,ab->ta', grad, weight, preferred_element_type=jnp.float32)  39.5 us
  transfers between devices with their start and end apart: 29, of which 21 were waited for; matrix products, arithmetic and copies ran while one was open for 28% of the time, Pallas kernels for 0%

profile of v1, /device:TPU:0, one launch (start us, length us, event | category | flops | bytes accessed | tf_op | source)
XLA Modules:
  0.0 1537.1 jit_solution(10068132202937804274)
XLA Ops:
  13.7 4.0 collective-permute-start.1
  24.3 38.8 %all-reduce.5 = (bf16[768]{0:T(1024)(128)(2,1)S(1)}, bf16[768]{0:T(1024)(128)(2,1)S(1)}) all-reduce(bf16[768]{0:T(1024)(128)(2,1)S(1)} %dynamic-update-slice, bf16[768]{0:T(1024)(128)(2,1)S(1)} %dynamic-update-slice.1), channel_id=6, replica_groups=mesh['dp'=2,'row'=4,'col'=4] {'row','col'}, use_global_device_ids=true, to_apply=%add | all-reduce | flops 1536 | bytes 6144
  66.6 5.4 collective-permute-start.3
  77.1 6.0 collective-permute-start.5
  83.1 3.4 collective-permute-done.4
  88.7 4.6 collective-permute-start.7
  93.3 3.3 collective-permute-done.6
  96.6 4.8 collective-permute-done.7
  106.0 8.7 collective-permute-done.9
  119.3 3.4 collective-permute-done.11
  128.2 5.3 collective-permute-start.14
  135.5 6.6 collective-permute-done.14
  152.7 4.5 fusion.54
  172.3 31.8 %all-gather.19.cloned.1.call-done = bf16[3072,192]{1,0:T(8,128)(2,1)} async-done(((bf16[192,192]{1,0:T(8,128)(2,1)}), bf16[3072,192]{1,0:T(8,128)(2,1)}) %all-gather.19.cloned.1.call-update) | async-done | bytes 1179664 | tf_op jit(solution)/shard_map/all_gather | solution.py:73
  208.2 4.5 convolution_convert_fusion.1
  212.6 4.3 copy.127
  216.9 56.9 %while.32 = (s32[]{:T(128)}, bf16[12,1024,64]{1,2,0:T(8,128)(2,1)S(1)}, f32[12,1024]{1,0:T(8,128)S(1)}, f32[12,1024]{1,0:T(8,128)S(1)}, bf16[12,1024,64]{2,1,0:T...) while((s32[]{:T(128)}, ...), condition=%wide.region_4.5_spmd.clone.clone, body=%wide.region_1.4_spmd.clone.sunk.clone | while | flops 279967744 | bytes 13678685 | solution.py:197
  279.3 3.8 multiply_reduce_fusion.4
  285.0 48.0 %all-gather.23.cloned.1.call-done = bf16[3072,512]{1,0:T(8,128)(2,1)} async-done(((bf16[192,512]{1,0:T(8,128)(2,1)}), bf16[3072,512]{1,0:T(8,128)(2,1)}) %all-gather.23.cloned.1.call-update) | async-done | bytes 3145744 | tf_op jit(solution)/shard_map/all_gather | solution.py:83
  333.0 4.3 copy.131
  340.0 65.3 %all-gather.25.cloned.1.call-done = bf16[8192,192]{0,1:T(8,128)(2,1)} async-done(((bf16[512,192]{0,1:T(8,128)(2,1)}), bf16[8192,192]{0,1:T(8,128)(2,1)}) %all-gather.25.cloned.1.call-update) | async-done | bytes 3145744 | tf_op jit(solution)/shard_map/all_gather | solution.py:85
  405.3 6.5 reshape.314
  417.3 3.6 fusion.73
  420.9 7.9 multiply_convert_fusion.3
  428.8 5.7 multiply_reduce_fusion.3
  437.3 12.6 multiply_convert_fusion.1
  450.0 5.5 fusion.74
  455.6 4.6 multiply_reduce_fusion.1
  464.9 3.5 fusion.77
  472.8 155.3 %while.33 = (s32[]{:T(128)}, f32[12,1024,64]{1,2,0:T(8,128)}, f32[12,1024,64]{1,2,0:T(8,128)}, bf16[12,1024,64]{1,2,0:T(8,128)(2,1)S(1)}, bf16[12,1024,64]{2,1,0...) while((s32[]{:T(128)}, f32[12,1024,64]{1,2,0:T(8,128)}, ...), condition=%wide.region_11.12_spmd.clone.clone, body=%wide.region_9.11_spmd.clone.sunk.clone | while | flops 689961984 | bytes 34129008 | solution.py:273
  474.6 3.3 multiply_reduce_fusion.7
  500.5 3.3 multiply_reduce_fusion.7
  513.4 3.3 multiply_reduce_fusion.7
  526.4 3.3 multiply_reduce_fusion.7
  539.3 3.3 multiply_reduce_fusion.7
  552.2 3.2 multiply_reduce_fusion.7
  565.2 3.3 multiply_reduce_fusion.7
  578.1 3.3 multiply_reduce_fusion.7
  591.1 3.3 multiply_reduce_fusion.7
  604.1 3.3 multiply_reduce_fusion.7
  617.0 3.3 multiply_reduce_fusion.7
  628.1 4.4 multiply_subtract_fusion.1
  637.3 4.9 reshape.317
  642.2 4.9 copy.141
  652.0 4.9 reshape.319
  656.9 4.8 copy.142
  665.9 3.7 reshape.321
  673.9 9.3 fusion.58
  683.2 8.5 reshape.328
  691.7 7.5 copy.147
  700.6 7.4 fusion.79
  708.0 8.4 reshape.326
  716.5 7.3 copy.145
  723.9 7.5 fusion.78
  731.3 8.4 reshape.324
  739.8 7.7 copy.144
  748.2 74.1 %all-reduce.4 = (bf16[16,48]{1,0:T(8,128)(2,1)S(1)}, bf16[16,48]{1,0:T(8,128)(2,1)S(1)}) all-reduce(f32[16,48]{1,0:T(8,128)S(1)} %reshape.330, f32[16,48]{1,0:T(8,128)S(1)} %reshape.331), channel_id=17, replica_groups=mesh['dp'=2,'row'=4,'col'=4] {'row','col'}, use_global_device_ids=true, to_apply=%region_27.28.clone | all-reduce | flops 1536 | bytes 9216
  832.6 78.4 %reduce-scatter.10.cloned.1.call-done = f32[1,192,192]{2,1,0:T(8,128)} async-done(((f32[16,192,192]{2,1,0:T(8,128)}), f32[1,192,192]{2,1,0:T(8,128)}) %reduce-scatter.10.cloned.1.call-update) | async-done | bytes 147472 | tf_op jit(solution)/shard_map/reduce_scatter | solution.py:311
  912.6 133.0 %reduce-scatter.12.cloned.1.call-done = f32[1,192,192]{2,1,0:T(8,128)} async-done(((f32[16,192,192]{2,1,0:T(8,128)}), f32[1,192,192]{2,1,0:T(8,128)}) %reduce-scatter.12.cloned.1.call-update) | async-done | bytes 147472 | tf_op jit(solution)/shard_map/reduce_scatter | solution.py:311
  1047.2 148.7 %reduce-scatter.20.cloned.1.call-done = f32[1,512,192]{1,2,0:T(8,128)} async-done(((f32[16,512,192]{1,2,0:T(8,128)}), f32[1,512,192]{1,2,0:T(8,128)}) %reduce-scatter.20.cloned.1.call-update) | async-done | bytes 393232 | tf_op jit(solution)/shard_map/reduce_scatter | solution.py:250
  1197.6 148.2 %reduce-scatter.18.cloned.1.call-done = f32[1,192,512]{2,1,0:T(8,128)} async-done(((f32[16,192,512]{2,1,0:T(8,128)}), f32[1,192,512]{2,1,0:T(8,128)}) %reduce-scatter.18.cloned.1.call-update) | async-done | bytes 393232 | tf_op jit(solution)/shard_map/reduce_scatter | solution.py:244
  1347.4 148.5 %reduce-scatter.16.cloned.1.call-done = f32[1,192,512]{2,1,0:T(8,128)} async-done(((f32[16,192,512]{2,1,0:T(8,128)}), f32[1,192,512]{2,1,0:T(8,128)}) %reduce-scatter.16.cloned.1.call-update) | async-done | bytes 393232 | tf_op jit(solution)/shard_map/reduce_scatter | solution.py:238
  1502.0 7.9 add_convert_fusion
  1514.1 4.8 all-reduce.10.cloned.1.call-done
  (380 shorter events, 330.3 us)
Async XLA Ops:
  7.2 140.2 %all-gather.17.cloned.1.call-start = ((), (), s32[]{:S(2)}) async-start(), calls=%async_computation.15 | async-start | bytes 1671168 | tf_op jit(solution)/shard_map/all_gather | solution.py:72
  7.9 149.3 %all-gather.15.cloned.1.call-start = ((), (), s32[]{:S(2)}) async-start(), calls=%async_computation.14 | async-start | bytes 1671168 | tf_op jit(solution)/shard_map/all_gather | solution.py:71
  8.7 195.4 %all-gather.19.cloned.1.call-start = ((), (), s32[]{:S(2)}) async-start(), calls=%async_computation.16 | async-start | bytes 1671168 | tf_op jit(solution)/shard_map/all_gather | solution.py:73
  9.4 264.5 %all-gather.21.cloned.1.call-start = ((), (), s32[]{:S(2)}) async-start(), calls=%async_computation.17 | async-start | bytes 1671168 | tf_op jit(solution)/shard_map/all_gather | solution.py:74
  10.0 323.0 %all-gather.23.cloned.1.call-start = ((), (), s32[]{:S(2)}) async-start(), calls=%async_computation.18 | async-start | bytes 3342336 | tf_op jit(solution)/shard_map/all_gather | solution.py:83
  10.6 394.7 %all-gather.25.cloned.1.call-start = ((), (), s32[]{:S(2)}) async-start(), calls=%async_computation.19 | async-start | bytes 3342336 | tf_op jit(solution)/shard_map/all_gather | solution.py:85
  10.6 55.8 %collective-permute-start = (bf16[1,192,512]{2,1,0:T(8,128)(2,1)}, bf16[1,192,512]{2,1,0:T(8,128)(2,1)}, u32[]{:S(2)}, u32[]{:S(2)}) collective-permute-start(bf16[1,192,512]{2,1,0:T(8,128)(2,1)} %bitcast.334), channel_id=1, source_target_pairs={{0,1},{1,2},{2,3},{3,4},{4,5},{5,6},{6,7},{7,8},{8,9},{9,10},{10,1... | collective-permute-start | bytes 589832 | tf_op jit(solution)/shard_map/ppermute | solution.py:27
  13.7 52.9 %collective-permute-start.1 = (bf16[1,192,512]{2,1,0:T(8,128)(2,1)}, bf16[1,192,512]{2,1,0:T(8,128)(2,1)}, u32[]{:S(2)}, u32[]{:S(2)}) collective-permute-start(bf16[1,192,512]{2,1,0:T(8,128)(2,1)} %bitcast.335), channel_id=1, source_target_pairs={{0,15},{1,0},{2,1},{3,2},{4,3},{5,4},{6,5},{7,6},{8,7},{9,8},{10,9... | collective-permute-start | bytes 589832 | tf_op jit(solution)/shard_map/ppermute | solution.py:32
  17.7 811.6 %reduce-scatter.14.cloned.1.call-start = ((), (), s32[]{:S(2)}) async-start(), calls=%async_computation.10 | async-start | bytes 3342336 | tf_op jit(solution)/shard_map/reduce_scatter | solution.py:311
  18.2 4.4 copy-start.2
  19.8 2.8 copy-start.46
  19.8 4.0 copy-start.47
  19.9 4.3 copy-start.48
  19.9 43.3 %copy-start.17 = (bf16[1024,768]{1,0:T(8,128)(2,1)S(1)}, bf16[1024,768]{1,0:T(8,128)(2,1)}, u32[]{:S(2)}) copy-start(bf16[1024,768]{1,0:T(8,128)(2,1)} %param.27) | copy-start | bytes 4718596
  63.2 397.0 %copy-start.37 = (f32[768]{0:T(1024)}, f32[768]{0:T(1024)S(1)}, u32[]{:S(2)}) copy-start(f32[768]{0:T(1024)S(1)} %convert_element_type.259) | copy-start | bytes 9220
  63.2 3.1 copy-start.36
  66.0 99.2 %copy-start.29 = (f32[1024,32]{0,1:T(8,128)}, f32[1024,32]{0,1:T(8,128)S(1)}, u32[]{:S(2)}) copy-start(f32[1024,32]{0,1:T(8,128)S(1)} %get-tuple-element.394) | copy-start | bytes 393220
  66.4 10.7 collective-permute-start.2
  66.6 10.5 collective-permute-start.3
  77.1 9.4 collective-permute-start.4
  77.1 11.6 collective-permute-start.5
  86.5 10.1 collective-permute-start.6
  88.7 12.8 collective-permute-start.7
  96.6 9.4 collective-permute-start.8
  101.4 13.3 collective-permute-start.9
  106.0 10.7 collective-permute-start.10
  114.7 8.0 collective-permute-start.11
  116.7 11.4 collective-permute-start.12
  122.7 12.8 collective-permute-start.13
  128.2 14.0 collective-permute-start.14
  147.3 5.4 copy-start.18
  162.4 2.9 copy-start.16
  208.2 4.5 copy-start.12
  212.6 4.3 copy-start.7
  212.6 4.3 copy-start.34
  273.8 5.5 copy-start.5
  283.1 177.1 %copy-start = (f32[1024,768]{0,1:T(8,128)}, f32[1024,768]{0,1:T(8,128)S(1)}, u32[]{:S(2)}) copy-start(f32[1024,768]{0,1:T(8,128)S(1)} %get-tuple-element.398) | copy-start | bytes 9437188
  283.2 177.1 %copy-start.39 = (f32[1024]{0:T(1024)}, f32[1024]{0:T(1024)S(1)}, u32[]{:S(2)}) copy-start(f32[1024]{0:T(1024)S(1)} %add_rsqrt_fusion.1) | copy-start | bytes 12292
  417.3 3.6 copy-start.14
  420.9 7.9 copy-start.49
  428.8 5.7 copy-start.9
  434.5 21.1 %copy-start.13 = (f32[1024,768]{0,1:T(8,128)}, f32[1024,768]{0,1:T(8,128)S(1)}, u32[]{:S(2)}) copy-start(f32[1024,768]{0,1:T(8,128)S(1)} %get-tuple-element.402) | copy-start | bytes 9437188
  437.3 18.2 %copy-start.44 = (f32[1024]{0:T(1024)}, f32[1024]{0:T(1024)S(1)}, u32[]{:S(2)}) copy-start(f32[1024]{0:T(1024)S(1)} %broadcast_multiply_fusion.1) | copy-start | bytes 12292
  450.0 5.6 copy-start.50
  468.5 4.3 copy-start.3
  468.5 362.6 %reduce-scatter.8.cloned.1.call-start = ((), (), s32[]{:S(2)}) async-start(), calls=%async_computation.7 | async-start | bytes 3342336 | tf_op jit(solution)/shard_map/reduce_scatter | solution.py:311
  472.8 155.3 %copy-start.30 = (f32[1024,32]{0,1:T(8,128)S(1)}, f32[1024,32]{0,1:T(8,128)}, u32[]{:S(2)}) copy-start(f32[1024,32]{0,1:T(8,128)} %copy-done.29) | copy-start | bytes 393220
  472.8 155.3 %copy-start.35 = (f32[1024,32]{0,1:T(8,128)S(1)}, f32[1024,32]{0,1:T(8,128)}, u32[]{:S(2)}) copy-start(f32[1024,32]{0,1:T(8,128)} %get-tuple-element.392) | copy-start | bytes 393220
  628.1 34.1 %copy-start.4 = (bf16[12,1024,64]{1,2,0:T(8,128)(2,1)}, bf16[12,1024,64]{1,2,0:T(8,128)(2,1)S(1)}, u32[]{:S(2)}) copy-start(bf16[12,1024,64]{1,2,0:T(8,128)(2,1)S(1)} %get-tuple-element.119) | copy-start | bytes 4718596
  647.1 263.9 %reduce-scatter.10.cloned.1.call-start = ((), (), s32[]{:S(2)}) async-start(), calls=%async_computation.8 | async-start | bytes 3342336 | tf_op jit(solution)/shard_map/reduce_scatter | solution.py:311
  661.7 383.9 %reduce-scatter.12.cloned.1.call-start = ((), (), s32[]{:S(2)}) async-start(), calls=%async_computation.9 | async-start | bytes 3342336 | tf_op jit(solution)/shard_map/reduce_scatter | solution.py:311
  672.5 523.3 %reduce-scatter.20.cloned.1.call-start = ((), (), s32[]{:S(2)}) async-start(), calls=%async_computation.13 | async-start | bytes 6684672 | tf_op jit(solution)/shard_map/reduce_scatter | solution.py:250
  699.2 646.5 %reduce-scatter.18.cloned.1.call-start = ((), (), s32[]{:S(2)}) async-start(), calls=%async_computation.12 | async-start | bytes 6684672 | tf_op jit(solution)/shard_map/reduce_scatter | solution.py:244
  723.8 772.1 %reduce-scatter.16.cloned.1.call-start = ((), (), s32[]{:S(2)}) async-start(), calls=%async_computation.11 | async-start | bytes 6684672 | tf_op jit(solution)/shard_map/reduce_scatter | solution.py:238
  747.5 75.4 %copy-start.23 = (bf16[1024,12,64]{0,2,1:T(8,128)(2,1)S(1)}, bf16[1024,12,64]{0,2,1:T(8,128)(2,1)}, u32[]{:S(2)}) copy-start(bf16[1024,12,64]{0,2,1:T(8,128)(2,1)} %copy-done.22) | copy-start | bytes 4718596
  747.5 75.4 %copy-start.32 = (bf16[768,768]{0,1:T(8,128)(2,1)S(1)}, bf16[768,768]{0,1:T(8,128)(2,1)}, u32[]{:S(2)}) copy-start(bf16[768,768]{0,1:T(8,128)(2,1)} %reshape.302) | copy-start | bytes 3538948
  747.5 771.4 %all-reduce.10.cloned.1.call-start = ((), (), s32[]{:S(2)}) async-start(), calls=%async_computation.20 | async-start | bytes 1966080 | tf_op jit(solution)/shard_map/psum | solution.py:317
  822.9 3.2 copy-start.25
  822.9 3.2 copy-start.31
  829.3 672.7 %copy-start.1 = (f32[1024,768]{0,1:T(8,128)S(1)}, f32[1024,768]{0,1:T(8,128)}, u32[]{:S(2)}) copy-start(f32[1024,768]{0,1:T(8,128)} %copy-done) | copy-start | bytes 9437188
  829.3 672.7 %copy-start.38 = (f32[768]{0:T(1024)S(1)}, f32[768]{0:T(1024)}, u32[]{:S(2)}) copy-start(f32[768]{0:T(1024)} %copy-done.37) | copy-start | bytes 9220
  829.3 672.7 %copy-start.40 = (f32[1024]{0:T(1024)S(1)}, f32[1024]{0:T(1024)}, u32[]{:S(2)}) copy-start(f32[1024]{0:T(1024)} %copy-done.39) | copy-start | bytes 12292
  829.3 672.7 %copy-start.42 = (f32[1024]{0:T(1024)S(1)}, f32[1024]{0:T(1024)}, u32[]{:S(2)}) copy-start(f32[1024]{0:T(1024)} %copy-done.41) | copy-start | bytes 12292
  1509.8 2.7 copy-start.11
  (16 other events, 26.3 us)
Sparse Core Ops, SparseCore 0:
  10.9 66.0 all-gather.16
  79.7 64.1 all-gather.14
  146.8 57.2 all-gather.18
  206.8 56.6 all-gather.20
  266.2 66.8 all-gather.22
  335.6 69.6 all-gather.24
  468.6 128.6 reduce-scatter.13
  647.2 128.7 reduce-scatter.7
  781.0 129.9 reduce-scatter.9
  915.8 129.7 reduce-scatter.11
  1050.8 144.9 reduce-scatter.19
  1200.9 144.7 reduce-scatter.17
  1350.9 144.9 reduce-scatter.15
  1499.8 19.0 all-reduce.9
